TPU v7x, 32 devices: a whole 2x2x4 slice. The times are simulated.
32 devices in a mesh: shot: 2 (over y), box: 8 (over z, x), sub: 2 (over core).
Axes of the slice: x: 2, y: 2, z: 4, core: 2. Of those that a mesh axis runs over, the one named last changes fastest.
Arguments:
- box_weights: float32 [64, 256, 128], P(('shot', 'box', 'sub')), parts along dimension 0, may hold values from -6 to 6
- velocity: float32 [8192], P('shot'), parts along dimension 0, may hold values from -4 to 4
- switch_kernel: float32 [128, 128], replicated, may hold values from -0.5 to 0.5
Outputs:
- final_weights: float32 [4, 4096, 128], P('shot', ('box', 'sub')), parts along dimension 0
There are 2 independent parts, one for each index of `shot`. A program takes and returns all parts, laid end to end along the dimension named above; an argument that names none is the same for every part. Nothing has to cross between parts.
All inputs are finite; a program needn't handle non-finite values.
Results may differ from a plain program's by a relative error of at most 0.00013.
Values sent between devices are 32-bit elements; how exact they have to be, the bound alone decides.
No kernel may reach another device: no remote copies, remote signals or barrier semaphores. Data moves between devices by JAX's collectives and lax.ppermute only.
A program may use at most 64 MiB of HBM per device.

v0:
```python
import jax
import jax.numpy as jnp
from jax import lax
from jax.sharding import PartitionSpec as P

CHEB = 8
half_root = 0.7071067811865476


def swapped(value, axis, apart):
    mask = 2**apart
    pairs = [(source, source ^ mask) for source in range(lax.axis_size(axis))]
    return lax.ppermute(value, axis, pairs)


def cheb_nodes():
    counter = jnp.arange(CHEB, dtype=jnp.float32)
    return jnp.cos(jnp.pi * (2.0 * counter + 1.0) / (2.0 * CHEB))


def lagrange_rows(points, node_values):
    differences = points[:, None] - node_values[None, :]
    node_gaps = node_values[:, None] - node_values[None, :]
    identity = jnp.eye(CHEB, dtype=jnp.float32)
    numerator = jnp.prod(
        jnp.where(identity[None, :, :] > 0.5, 1.0, differences[:, None, :]), axis=2
    )
    denominator = jnp.prod(jnp.where(identity > 0.5, 1.0, node_gaps), axis=1)
    return numerator / denominator[None, :]


def spread_coord(values, axis_dim):
    if axis_dim == 0:
        return jnp.repeat(values, CHEB)
    return jnp.tile(values, CHEB)


def level_tables(axis_dim):
    node_values = cheb_nodes()
    identity = jnp.eye(CHEB, dtype=jnp.float32)
    pair_eye = jnp.eye(2, dtype=jnp.float32)
    matrices = []
    coords = []
    for child_idx in (0, 1):
        child_pts = (node_values + (2.0 * child_idx - 1.0)) * 0.5
        lagrange = lagrange_rows(child_pts, node_values)
        if axis_dim == 0:
            single = jnp.kron(lagrange, identity)
        else:
            single = jnp.kron(identity, lagrange)
        matrices.append(jnp.kron(pair_eye, single))
        coords.append(spread_coord(child_pts, axis_dim))
    return (jnp.concatenate(matrices, 0), jnp.stack(coords), spread_coord(node_values, axis_dim))


def rotate(values, angles):
    real_part = values[..., : CHEB * CHEB]
    imag_part = values[..., CHEB * CHEB :]
    cosines = jnp.cos(angles)
    sine_vals = jnp.sin(angles)
    return jnp.concatenate(
        [real_part * cosines - imag_part * sine_vals, real_part * sine_vals + imag_part * cosines],
        -1,
    )


def merge_blocks(blocks, omegas, weights, coord_in, coord_out):
    phase = omegas[None, None, :, :, None]
    first_term = rotate(blocks[:, 0][:, :, None], -phase * coord_in[0])
    second_term = rotate(blocks[:, 1][:, :, None], -phase * coord_in[1])
    joined = jnp.concatenate([first_term, second_term], -1)
    mixture = jnp.dot(
        joined.reshape(-1, 4 * CHEB * CHEB),
        weights,
        precision=lax.Precision.HIGHEST,
        preferred_element_type=jnp.float32,
    )
    mixture = mixture.reshape(first_term.shape)
    return rotate(mixture, phase * coord_out) * half_root


def apply_switch(current, switch_kernel):
    flat = jnp.dot(
        current.reshape(-1, current.shape[-1]),
        switch_kernel,
        precision=lax.Precision.HIGHEST,
        preferred_element_type=jnp.float32,
    )
    return flat.reshape(current.shape)


def level_omegas(velocity, device, level_idx, tgt_count):
    tgt_code = device % 2 ** (level_idx + 1)
    return lax.dynamic_slice_in_dim(velocity, tgt_code * tgt_count, tgt_count)


def own_part(current, omegas, my_child, level_idx):
    vec_len = current.shape[-1]
    weights, coord_in, coord_out = level_tables(level_idx % 2)
    coord_mine = jnp.where(my_child == 0, coord_in[0], coord_in[1])
    weight_mine = jnp.where(my_child == 0, weights[:vec_len], weights[vec_len:])
    turned = rotate(current, -omegas[None, :, None] * coord_mine[None, None, :])
    return jnp.dot(
        turned.reshape(-1, vec_len),
        weight_mine,
        precision=lax.Precision.HIGHEST,
        preferred_element_type=jnp.float32,
    )


def far_part(own_term, partner, omegas, my_child, level_idx):
    vec_len = partner.shape[-1]
    weights, coord_in, coord_out = level_tables(level_idx % 2)
    coord_other = jnp.where(my_child == 0, coord_in[1], coord_in[0])
    weight_other = jnp.where(my_child == 0, weights[vec_len:], weights[:vec_len])
    turned = rotate(partner, -omegas[None, :, None] * coord_other[None, None, :])
    far_term = jnp.dot(
        turned.reshape(-1, vec_len),
        weight_other,
        precision=lax.Precision.HIGHEST,
        preferred_element_type=jnp.float32,
    )
    mixture = (own_term + far_term).reshape(partner.shape)
    return rotate(mixture, omegas[None, :, None] * coord_out[None, None, :]) * half_root


def body(box_weights, velocity, switch_kernel):
    box_count = lax.axis_size("box")
    sub_count = lax.axis_size("sub")
    box_bits = box_count.bit_length() - 1
    sub_bits = sub_count.bit_length() - 1
    levels = box_bits + sub_bits
    box_index = lax.axis_index("box")
    sub_index = lax.axis_index("sub")
    device = box_index * sub_count + sub_index
    src_count = box_weights.shape[0]
    tgt_count = box_weights.shape[1]
    vec_len = box_weights.shape[2]
    current = box_weights
    bit_idx = 0
    level_idx = bit_idx
    my_child = sub_index // 2**bit_idx % 2
    omegas = level_omegas(velocity, device, level_idx, tgt_count)
    own_term = own_part(current, omegas, my_child, level_idx)
    partner = swapped(current, "sub", bit_idx)
    current = far_part(own_term, partner, omegas, my_child, level_idx)
    spread = lax.all_to_all(current, "box", split_axis=1, concat_axis=0, tiled=True)
    block_width = tgt_count // box_count
    for bit_idx in range(box_bits):
        level_idx = sub_bits + bit_idx
        weights, coord_in, coord_out = level_tables(level_idx % 2)
        row_count = spread.shape[0]
        col_count = spread.shape[1]
        groups = 2 ** (bit_idx + 1)
        vel_table = velocity[: sub_count * groups * tgt_count].reshape(groups, sub_count, tgt_count)
        omegas = lax.dynamic_slice(
            vel_table, (0, sub_index, box_index * block_width), (groups, 1, block_width)
        )
        omegas = omegas.reshape(2, col_count)
        blocks = spread.reshape(row_count // (2 * src_count), 2, src_count, col_count, vec_len)
        merged = merge_blocks(blocks, omegas, weights, coord_in, coord_out)
        spread = merged.reshape(row_count // 2, 2 * col_count, vec_len)
        if level_idx == levels // 2 - 1:
            spread = apply_switch(spread, switch_kernel)
    current = lax.all_to_all(spread, "box", split_axis=1, concat_axis=1, tiled=True)
    return current


def solution(mesh):
    return jax.shard_map(
        body,
        mesh=mesh,
        in_specs=(P(("shot", "box", "sub"), None, None), P("shot"), P()),
        out_specs=P("shot", ("box", "sub"), None),
        check_vma=False,
    )
```

profile of v0, /device:TPU:0, one launch (start us, length us, event | category | flops | bytes accessed | tf_op | source)
XLA Modules:
  0.0 46.1 jit_solution(10633600639100690880)
XLA Ops:
  0.0 0.5 %collective-permute-start = (f32[2,256,128]{2,1,0:T(8,128)}, f32[2,256,128]{2,1,0:T(8,128)S(1)}, u32[]{:S(2)}, u32[]{:S(2)}) collective-permute-start(f32[2,256,128]{2,1,0:T(8,128)} %param.3), channel_id=1, source_target_pairs={{0,1},{1,0},{2,3},{3,2},{4,5},{5,4},{6,7},{7,6},{8,9},{9,8},{10,11... | collective-permute-start | bytes 786440 | tf_op jit(solution)/shard_map/ppermute | solution.py:13
  0.7 0.7 %copy-done.2 = f32[4096]{0:T(1024)S(1)} copy-done((f32[4096]{0:T(1024)S(1)}, f32[4096]{0:T(1024)}, u32[]{:S(2)}) %copy-start.2) | copy-done | bytes 16408
  1.6 0.1 squeeze_stack_reshape.16
  1.8 0.2 select_reduce_fusion.2
  2.0 0.3 select_reduce_fusion.1
  2.3 0.1 broadcast_multiply_fusion
  2.5 0.1 mul.1285
  2.6 0.1 mul.1290
  2.8 0.1 mul.1344
  2.9 0.1 mul.1350
  3.2 0.5 %slice-done.1 = f32[2048]{0:T(1024)S(1)} async-done(((f32[4096]{0:T(1024)}), f32[2048]{0:T(1024)S(1)}, s32[]{:S(2)}) %slice-start.1) | async-done | bytes 8216 | tf_op jit(solution)/shard_map/slice | solution.py:155
  3.7 0.1 dynamic-slice_reduce_fusion.1
  3.8 0.1 broadcast_in_dim_reshape.12
  3.9 0.3 multiply_cosine_fusion.5
  4.2 0.3 multiply_cosine_fusion.8
  4.6 0.4 slice-done
  5.2 0.3 broadcast_select_fusion
  5.5 0.1 mul.1347
  5.7 0.1 mul.1353
  5.9 0.5 %multiply_cosine_fusion.7 = (f32[2,64,64]{2,1,0:T(8,128)S(1)}, f32[2,64,64]{2,1,0:T(8,128)S(1)}, f32[2,64,64]{2,1,0:T(8,128)S(1)}, f32[2,64,64]{2,1,0:T(8,128)S(1)}) fusion(f32[64]{0:T(128)S(1)} %squeeze_stack_reshape.16, f32[2,64]{1,0:T(2,128)S(1)} %neg.34, f32[64]{0:T(128)S(1)} %squeeze_stack_reshape.17), kind=kLoop, calls=%fused_computation.103 | loop fusion | flops 16384 | bytes 132096 | tf_op jit(solution)/shard_map/cos | solution.py:59
  6.4 0.1 dynamic-slice_reduce_fusion
  6.6 1.0 %multiply_cosine_fusion.2 = (f32[256,64]{1,0:T(8,128)S(1)}, f32[256,64]{1,0:T(8,128)S(1)}, f32[256,64]{1,0:T(8,128)S(1)}, f32[256,64]{1,0:T(8,128)S(1)}) fusion(f32[64]{0:T(128)S(1)} %get-tuple-element.97, f32[256]{0:T(256)S(1)} %get-tuple-element.7, f32[64]{0:T(128)S(1)} %get-tuple-element.98), kind=kLoop, calls=%fused_computation.59 | loop fusion | flops 32768 | bytes 263680 | tf_op jit(solution)/shard_map/cos | solution.py:59
  7.6 0.2 multiply_subtract_fusion.9
  7.8 0.1 pad_maximum_fusion
  7.9 0.3 multiply_cosine_fusion.4
  8.2 0.3 multiply_cosine_fusion.11
  8.6 0.1 select_n.114
  8.7 0.1 select_n.117
  8.8 0.1 mul.1391
  8.9 0.1 mul.1392
  9.1 0.4 fusion.39
  9.5 0.2 multiply_subtract_fusion.8
  9.6 0.1 pad_maximum_fusion.1
  9.8 0.4 convolution_add_fusion
  10.1 0.1 fusion.38
  10.3 0.1 copy.42
  10.4 0.1 copy.43
  10.6 0.8 %copy.29 = f32[2,256,128]{2,0,1:T(2,128)} copy(f32[2,256,128]{1,2,0:T(8,128)S(1)} %maximum_multiply_fusion) | data formatting | bytes 524288 | tf_op jit(solution)/shard_map/mul | solution.py:124
  11.4 6.8 %all-to-all-start = ((f32[2,256,128]{2,0,1:T(2,128)}), f32[2,256,128]{2,0,1:T(2,128)S(1)}, u32[]{:S(2)}, u32[]{:S(2)}) async-start(f32[2,256,128]{2,0,1:T(2,128)} %copy.29), calls=%async_computation | async-start | bytes 524288 | tf_op jit(solution)/shard_map/all_to_all | solution.py:147
  18.2 0.2 multiply_cosine_fusion.9
  18.4 1.0 %multiply_cosine_fusion.1 = (f32[2,128,64]{2,1,0:T(8,128)S(1)}, f32[2,128,64]{2,1,0:T(8,128)S(1)}, f32[2,128,64]{2,1,0:T(8,128)S(1)}, f32[2,128,64]{2,1,0:T(8,128)S(1)}) fusion(f32[64]{0:T(128)S(1)} %mul.1317, f32[2,128]{1,0:T(2,128)S(1)} %neg.35, f32[64]{0:T(128)S(1)} %mul.1330), kind=kLoop, calls=%fused_computation.57 | loop fusion | flops 32768 | bytes 263680 | tf_op jit(solution)/shard_map/cos | solution.py:59
  19.4 8.4 %all-to-all-done = f32[2,256,128]{2,0,1:T(2,128)S(1)} async-done(((f32[2,256,128]{2,0,1:T(2,128)}), f32[2,256,128]{2,0,1:T(2,128)S(1)}, u32[]{:S(2)}, u32[]{:S(2)}) %all-to-all-start) | async-done | bytes 262176 | tf_op jit(solution)/shard_map/all_to_all | solution.py:147
  27.9 0.1 slice_bitcast_fusion.16
  28.0 0.1 slice_bitcast_fusion.13
  28.1 0.1 multiply_subtract_fusion.7
  28.3 0.7 %fusion = f32[4,2,2,32,128]{4,3,2,1,0:T(8,128)S(1)} fusion(f32[4,2,2,32,64]{4,3,2,1,0:T(8,128)S(1)} %get-tuple-element.32, f32[4,2,2,32,64]{4,3,2,1,0:T(8,128)S(1)} %get-tuple-element.31, f32[4,2,2,32,64]{4,3,2,1,0:T(8,128)S(1)} %get-tuple-element.30, f32[4,2,2,32,64]{4,3,2,1,0:T(8,128)S(1)} %get-tuple-element.29, ...), kind=kOutput, calls=%fused_computation.2 | convolution fusion | flops 201719808 | bytes 917504 | tf_op jit(solution)/shard_map/dot_general | solution.py:72
  28.9 0.2 multiply_subtract_fusion.5
  29.1 0.4 fusion.22
  29.6 0.1 slice_bitcast_fusion.10
  29.7 0.1 slice_bitcast_fusion.7
  29.9 0.7 %fusion.8 = f32[2,2,2,64,128]{4,3,2,1,0:T(8,128)S(1)} fusion(f32[2,2,2,64,64]{4,3,2,1,0:T(8,128)S(1)} %get-tuple-element.24, f32[2,2,2,64,64]{4,3,2,1,0:T(8,128)S(1)} %get-tuple-element.23, f32[2,2,2,64,64]{4,3,2,1,0:T(8,128)S(1)} %get-tuple-element.22, f32[2,2,2,64,64]{4,3,2,1,0:T(8,128)S(1)} %get-tuple-element.21, f32[128,128]{1,0:T(8,128)S(1)} %mul.1392, ...), kind=kOutput, calls=%fused_computation.10 | convolution fusion | flops 201752576 | bytes 917504 | tf_op jit(solution)/shard_map/dot_general | solution.py:72
  30.6 0.2 multiply_subtract_fusion.2
  30.8 0.1 maximum_multiply_fusion.3
  30.9 0.1 slice_bitcast_fusion.4
  31.0 0.1 slice_bitcast_fusion.1
  31.1 0.1 multiply_subtract_fusion
  31.3 0.9 %convolution_bitcast_fusion = f32[1,2,2,128,128]{3,4,2,1,0:T(8,128)S(1)} fusion(f32[1,2,2,128,64]{4,3,2,1,0:T(8,128)S(1)} %get-tuple-element.12, f32[1,2,2,128,64]{4,3,2,1,0:T(8,128)S(1)} %get-tuple-element.11, f32[1,2,2,128,64]{4,3,2,1,0:T(8,128)S(1)} %get-tuple-element.104, f32[1,2,2,128,64]{4,3,2,1,0:T(8,128)S(1)} %get-tuple-element.105, ...), kind=kOutput, calls=%fused_computation | convolution fusion | flops 201719808 | bytes 917504 | tf_op jit(solution)/shard_map/dot_general | solution.py:72
  32.2 0.1 copy.33
  32.3 0.1 concatenate.78
  32.4 0.1 copy.34
  32.5 0.1 concatenate.79
  32.7 0.1 copy.35
  32.8 12.5 %all_to_all.20 = f32[2,256,128]{2,0,1:T(2,128)S(1)} all-to-all(f32[2,256,128]{2,0,1:T(2,128)S(1)} %copy.35), channel_id=1, replica_groups=mesh['shot'=2,'box'=8,'sub'=2] {'box'}, dimensions={1} | all-to-all | bytes 524288 | tf_op jit(solution)/shard_map/all_to_all | solution.py:165
  45.3 0.7 %copy.36 = f32[2,256,128]{2,1,0:T(8,128)} copy(f32[2,256,128]{2,0,1:T(2,128)S(1)} %all_to_all.20) | data formatting | bytes 524288 | tf_op jit(solution)/shard_map/all_to_all | solution.py:165
  (50 shorter events, 1.5 us)
Async XLA Ops:
  0.0 29.1 %copy-start = (f32[128,128]{1,0:T(8,128)S(1)}, f32[128,128]{1,0:T(8,128)}, u32[]{:S(2)}) copy-start(f32[128,128]{1,0:T(8,128)} %param.5) | copy-start | bytes 196612
  0.0 9.4 %collective-permute-start = (f32[2,256,128]{2,1,0:T(8,128)}, f32[2,256,128]{2,1,0:T(8,128)S(1)}, u32[]{:S(2)}, u32[]{:S(2)}) collective-permute-start(f32[2,256,128]{2,1,0:T(8,128)} %param.3), channel_id=1, source_target_pairs={{0,1},{1,0},{2,3},{3,2},{4,5},{5,4},{6,7},{7,6},{8,9},{9,8},{10,11... | collective-permute-start | bytes 786440 | tf_op jit(solution)/shard_map/ppermute | solution.py:13
  0.7 0.7 %copy-start.2 = (f32[4096]{0:T(1024)S(1)}, f32[4096]{0:T(1024)}, u32[]{:S(2)}) copy-start(f32[4096]{0:T(1024)} %param.4) | copy-start | bytes 49156
  3.0 0.7 %slice-start.1 = ((f32[4096]{0:T(1024)}), f32[2048]{0:T(1024)S(1)}, s32[]{:S(2)}) async-start(f32[4096]{0:T(1024)} %param.4), calls=%async_computation.3 | async-start | bytes 16384 | tf_op jit(solution)/shard_map/slice | solution.py:155
  4.2 0.7 %slice-start = ((f32[4096]{0:T(1024)}), f32[1024]{0:T(1024)S(1)}, s32[]{:S(2)}) async-start(f32[4096]{0:T(1024)} %param.4), calls=%async_computation.2 | async-start | bytes 8192 | tf_op jit(solution)/shard_map/slice | solution.py:155
  6.6 1.0 %copy-start.1 = (f32[2,256,128]{2,1,0:T(8,128)S(1)}, f32[2,256,128]{2,1,0:T(8,128)}, u32[]{:S(2)}) copy-start(f32[2,256,128]{2,1,0:T(8,128)} %param.3) | copy-start | bytes 786436
  11.4 16.4 %all-to-all-start = ((f32[2,256,128]{2,0,1:T(2,128)}), f32[2,256,128]{2,0,1:T(2,128)S(1)}, u32[]{:S(2)}, u32[]{:S(2)}) async-start(f32[2,256,128]{2,0,1:T(2,128)} %copy.29), calls=%async_computation | async-start | bytes 524288 | tf_op jit(solution)/shard_map/all_to_all | solution.py:147
where the time goes:
time: 46.4 us; the launch traced here: 46.1 us
  blocking collectives  12.5 us (27%)
  waiting for transfers between devices  8.38 us (18%)
  starting transfers between devices  7.3 us (16%)
  local copies, waits for them, and re-layouts  7.19 us (15%)
  other arithmetic  6.78 us (15%)
  matrix products  3.37 us (7%)
  between operations  0.55 us (1%)
    all_to_all x1, blocking collectives, body(): lax.all_to_all(spread, 'box', split_axis=1, concat_axis=1, tiled=True)  12.5 us
    all_to_all x1, waiting for transfers between devices, body(): lax.all_to_all(current, 'box', split_axis=1, concat_axis=0, tiled=True)  8.38 us
    all_to_all x1, starting transfers between devices, body(): lax.all_to_all(current, 'box', split_axis=1, concat_axis=0, tiled=True)  6.81 us
    cos x8, other arithmetic, rotate(): cosines = jnp.cos(angles)  3.91 us
    dot_general x3, matrix products, merge_blocks(): jnp.dot(joined.reshape(-1, 4 * CHEB * CHEB), weights, precision=lax.Preci...  2.23 us
    sub x11, other arithmetic, rotate(): real_part * cosines - imag_part * sine_vals  1.13 us
    unnamed x9, local copies, waits for them, and re-layouts  0.93 us
    slice x6, local copies, waits for them, and re-layouts, body(): velocity[:sub_count * groups * tgt_count]  0.93 us
  transfers between devices with their start and end apart: 2, of which 1 were waited for; matrix products, arithmetic and copies ran while one was open for 18% of the time, Pallas kernels for 0%

commit v1 on v0

--- a/solution.py
+++ b/solution.py
@@ -162,7 +162,10 @@
         spread = merged.reshape(row_count // 2, 2 * col_count, vec_len)
         if level_idx == levels // 2 - 1:
             spread = apply_switch(spread, switch_kernel)
-    current = lax.all_to_all(spread, "box", split_axis=1, concat_axis=1, tiled=True)
+    n_dev = lax.axis_size("box")
+    pieces = jnp.stack(jnp.split(spread, n_dev, axis=1), axis=0)
+    pieces = lax.all_to_all(pieces, "box", split_axis=0, concat_axis=0)
+    current = jnp.concatenate(pieces, axis=1)
     return current
 
 

time: 46.4 us -> 47.3 us (1.019)
  local copies, waits for them, and re-layouts: 7.19 us -> 7.95 us
    another operation x0 -> x10, local copies, waits for them, and re-layouts: none -> 0.86 us  [body(): pieces = jnp.stack(jnp.split(spread, n_dev, axis=1), axis=0)]
    unnamed x9 -> x16, local copies, waits for them, and re-layouts: 0.93 us -> 0.98 us
where the time goes in v1:
time: 47.3 us; the launch traced here: 46.9 us
  blocking collectives  12.5 us (26%)
  waiting for transfers between devices  8.39 us (18%)
  local copies, waits for them, and re-layouts  7.95 us (17%)
  starting transfers between devices  7.3 us (15%)
  other arithmetic  6.78 us (14%)
  matrix products  3.36 us (7%)
  between operations  0.61 us (1%)
    all_to_all x1, blocking collectives, body(): pieces = lax.all_to_all(pieces, 'box', split_axis=0, concat_axis=0)  12.5 us
    all_to_all x1, waiting for transfers between devices, body(): lax.all_to_all(current, 'box', split_axis=1, concat_axis=0, tiled=True)  8.39 us
    all_to_all x1, starting transfers between devices, body(): lax.all_to_all(current, 'box', split_axis=1, concat_axis=0, tiled=True)  6.81 us
    cos x8, other arithmetic, rotate(): cosines = jnp.cos(angles)  3.91 us
    dot_general x3, matrix products, merge_blocks(): jnp.dot(joined.reshape(-1, 4 * CHEB * CHEB), weights, precision=lax.Preci...  2.22 us
    sub x11, other arithmetic, rotate(): real_part * cosines - imag_part * sine_vals  1.13 us
    unnamed x16, local copies, waits for them, and re-layouts  0.98 us
  transfers between devices with their start and end apart: 2, of which 1 were waited for; matrix products, arithmetic and copies ran while one was open for 18% of the time, Pallas kernels for 0%

profile of v1, /device:TPU:0, one launch (start us, length us, event | category | flops | bytes accessed | tf_op | source)
XLA Modules:
  0.0 46.9 jit_solution(17246111410913480117)
XLA Ops:
  0.0 0.5 %collective-permute-start = (f32[2,256,128]{2,1,0:T(8,128)}, f32[2,256,128]{2,1,0:T(8,128)S(1)}, u32[]{:S(2)}, u32[]{:S(2)}) collective-permute-start(f32[2,256,128]{2,1,0:T(8,128)} %param.3), channel_id=1, source_target_pairs={{0,1},{1,0},{2,3},{3,2},{4,5},{5,4},{6,7},{7,6},{8,9},{9,8},{10,11... | collective-permute-start | bytes 786440 | tf_op jit(solution)/shard_map/ppermute | solution.py:13
  0.7 0.7 %copy-done.2 = f32[4096]{0:T(1024)S(1)} copy-done((f32[4096]{0:T(1024)S(1)}, f32[4096]{0:T(1024)}, u32[]{:S(2)}) %copy-start.2) | copy-done | bytes 16408
  1.6 0.1 squeeze_stack_reshape.16
  1.8 0.2 select_reduce_fusion.2
  2.0 0.3 select_reduce_fusion.1
  2.3 0.1 broadcast_multiply_fusion
  2.5 0.1 mul.1285
  2.6 0.1 mul.1290
  2.8 0.1 mul.1344
  2.9 0.1 mul.1350
  3.2 0.5 %slice-done.1 = f32[2048]{0:T(1024)S(1)} async-done(((f32[4096]{0:T(1024)}), f32[2048]{0:T(1024)S(1)}, s32[]{:S(2)}) %slice-start.1) | async-done | bytes 8216 | tf_op jit(solution)/shard_map/slice | solution.py:155
  3.7 0.1 dynamic-slice_reduce_fusion.1
  3.8 0.1 broadcast_in_dim_reshape.12
  3.9 0.3 multiply_cosine_fusion.5
  4.2 0.3 multiply_cosine_fusion.8
  4.6 0.4 slice-done
  5.2 0.3 broadcast_select_fusion
  5.5 0.1 mul.1347
  5.7 0.1 mul.1353
  5.9 0.5 %multiply_cosine_fusion.7 = (f32[2,64,64]{2,1,0:T(8,128)S(1)}, f32[2,64,64]{2,1,0:T(8,128)S(1)}, f32[2,64,64]{2,1,0:T(8,128)S(1)}, f32[2,64,64]{2,1,0:T(8,128)S(1)}) fusion(f32[64]{0:T(128)S(1)} %squeeze_stack_reshape.16, f32[2,64]{1,0:T(2,128)S(1)} %neg.34, f32[64]{0:T(128)S(1)} %squeeze_stack_reshape.17), kind=kLoop, calls=%fused_computation.111 | loop fusion | flops 16384 | bytes 132096 | tf_op jit(solution)/shard_map/cos | solution.py:59
  6.4 0.1 dynamic-slice_reduce_fusion
  6.6 1.0 %multiply_cosine_fusion.2 = (f32[256,64]{1,0:T(8,128)S(1)}, f32[256,64]{1,0:T(8,128)S(1)}, f32[256,64]{1,0:T(8,128)S(1)}, f32[256,64]{1,0:T(8,128)S(1)}) fusion(f32[64]{0:T(128)S(1)} %get-tuple-element.105, f32[256]{0:T(256)S(1)} %get-tuple-element.7, f32[64]{0:T(128)S(1)} %get-tuple-element.106), kind=kLoop, calls=%fused_computation.59 | loop fusion | flops 32768 | bytes 263680 | tf_op jit(solution)/shard_map/cos | solution.py:59
  7.6 0.2 multiply_subtract_fusion.9
  7.8 0.1 pad_maximum_fusion
  7.9 0.3 multiply_cosine_fusion.4
  8.2 0.3 multiply_cosine_fusion.11
  8.6 0.1 select_n.114
  8.7 0.1 select_n.117
  8.8 0.1 mul.1391
  8.9 0.1 mul.1392
  9.1 0.4 fusion.39
  9.5 0.2 multiply_subtract_fusion.8
  9.6 0.1 pad_maximum_fusion.1
  9.8 0.4 convolution_add_fusion
  10.1 0.1 fusion.38
  10.3 0.1 copy.66
  10.4 0.1 copy.67
  10.6 0.8 %copy.46 = f32[2,256,128]{2,0,1:T(2,128)} copy(f32[2,256,128]{1,2,0:T(8,128)S(1)} %maximum_multiply_fusion) | data formatting | bytes 524288 | tf_op jit(solution)/shard_map/mul | solution.py:124
  11.4 6.8 %all-to-all-start = ((f32[2,256,128]{2,0,1:T(2,128)}), f32[2,256,128]{2,0,1:T(2,128)S(1)}, u32[]{:S(2)}, u32[]{:S(2)}) async-start(f32[2,256,128]{2,0,1:T(2,128)} %copy.46), calls=%async_computation | async-start | bytes 524288 | tf_op jit(solution)/shard_map/all_to_all | solution.py:147
  18.2 0.2 multiply_cosine_fusion.9
  18.4 1.0 %multiply_cosine_fusion.1 = (f32[2,128,64]{2,1,0:T(8,128)S(1)}, f32[2,128,64]{2,1,0:T(8,128)S(1)}, f32[2,128,64]{2,1,0:T(8,128)S(1)}, f32[2,128,64]{2,1,0:T(8,128)S(1)}) fusion(f32[64]{0:T(128)S(1)} %mul.1317, f32[2,128]{1,0:T(2,128)S(1)} %neg.35, f32[64]{0:T(128)S(1)} %mul.1330), kind=kLoop, calls=%fused_computation.57 | loop fusion | flops 32768 | bytes 263680 | tf_op jit(solution)/shard_map/cos | solution.py:59
  19.4 8.4 %all-to-all-done = f32[2,256,128]{2,0,1:T(2,128)S(1)} async-done(((f32[2,256,128]{2,0,1:T(2,128)}), f32[2,256,128]{2,0,1:T(2,128)S(1)}, u32[]{:S(2)}, u32[]{:S(2)}) %all-to-all-start) | async-done | bytes 262176 | tf_op jit(solution)/shard_map/all_to_all | solution.py:147
  27.9 0.1 slice_bitcast_fusion.24
  28.0 0.1 slice_bitcast_fusion.21
  28.1 0.1 multiply_subtract_fusion.7
  28.3 0.7 %fusion = f32[4,2,2,32,128]{4,3,2,1,0:T(8,128)S(1)} fusion(f32[4,2,2,32,64]{4,3,2,1,0:T(8,128)S(1)} %get-tuple-element.32, f32[4,2,2,32,64]{4,3,2,1,0:T(8,128)S(1)} %get-tuple-element.31, f32[4,2,2,32,64]{4,3,2,1,0:T(8,128)S(1)} %get-tuple-element.30, f32[4,2,2,32,64]{4,3,2,1,0:T(8,128)S(1)} %get-tuple-element.29, ...), kind=kOutput, calls=%fused_computation.2 | convolution fusion | flops 201719808 | bytes 917504 | tf_op jit(solution)/shard_map/dot_general | solution.py:72
  28.9 0.2 multiply_subtract_fusion.5
  29.1 0.4 fusion.22
  29.6 0.1 slice_bitcast_fusion.18
  29.7 0.1 slice_bitcast_fusion.15
  29.9 0.7 %fusion.8 = f32[2,2,2,64,128]{4,3,2,1,0:T(8,128)S(1)} fusion(f32[2,2,2,64,64]{4,3,2,1,0:T(8,128)S(1)} %get-tuple-element.24, f32[2,2,2,64,64]{4,3,2,1,0:T(8,128)S(1)} %get-tuple-element.23, f32[2,2,2,64,64]{4,3,2,1,0:T(8,128)S(1)} %get-tuple-element.22, f32[2,2,2,64,64]{4,3,2,1,0:T(8,128)S(1)} %get-tuple-element.21, f32[128,128]{1,0:T(8,128)S(1)} %mul.1392, ...), kind=kOutput, calls=%fused_computation.10 | convolution fusion | flops 201752576 | bytes 917504 | tf_op jit(solution)/shard_map/dot_general | solution.py:72
  30.6 0.2 multiply_subtract_fusion.2
  30.8 0.1 maximum_multiply_fusion.3
  30.9 0.1 slice_bitcast_fusion.12
  31.0 0.1 slice_bitcast_fusion.9
  31.1 0.1 multiply_subtract_fusion
  31.3 0.9 %convolution_bitcast_fusion = f32[1,2,2,128,128]{3,4,2,1,0:T(8,128)S(1)} fusion(f32[1,2,2,128,64]{4,3,2,1,0:T(8,128)S(1)} %get-tuple-element.12, f32[1,2,2,128,64]{4,3,2,1,0:T(8,128)S(1)} %get-tuple-element.11, f32[1,2,2,128,64]{4,3,2,1,0:T(8,128)S(1)} %get-tuple-element.112, f32[1,2,2,128,64]{4,3,2,1,0:T(8,128)S(1)} %get-tuple-element.113, ...), kind=kOutput, calls=%fused_computation | convolution fusion | flops 201719808 | bytes 917504 | tf_op jit(solution)/shard_map/dot_general | solution.py:72
  32.2 0.1 copy.50
  32.3 0.1 concatenate.78
  32.4 0.1 copy.51
  32.5 0.1 concatenate.79
  32.7 0.3 slice_bitcast_fusion
  33.7 12.5 %all_to_all.20 = f32[8,2,32,128]{3,2,1,0:T(8,128)S(1)} all-to-all(f32[8,2,32,128]{3,2,1,0:T(8,128)S(1)} %constant_dynamic-update-slice_fusion.2), channel_id=1, replica_groups=mesh['shot'=2,'box'=8,'sub'=2] {'box'}, dimensions={0} | all-to-all | bytes 524288 | tf_op jit(solution)/shard_map/all_to_all | solution.py:167
  46.2 0.7 %copy.60 = f32[8,2,32,128]{3,2,0,1:T(8,128)} copy(f32[8,2,32,128]{3,2,1,0:T(8,128)S(1)} %all_to_all.20) | data formatting | bytes 524288 | tf_op jit(solution)/shard_map/all_to_all | solution.py:167
  (66 shorter events, 2.2 us)
Async XLA Ops:
  0.0 29.1 %copy-start = (f32[128,128]{1,0:T(8,128)S(1)}, f32[128,128]{1,0:T(8,128)}, u32[]{:S(2)}) copy-start(f32[128,128]{1,0:T(8,128)} %param.5) | copy-start | bytes 196612
  0.0 9.4 %collective-permute-start = (f32[2,256,128]{2,1,0:T(8,128)}, f32[2,256,128]{2,1,0:T(8,128)S(1)}, u32[]{:S(2)}, u32[]{:S(2)}) collective-permute-start(f32[2,256,128]{2,1,0:T(8,128)} %param.3), channel_id=1, source_target_pairs={{0,1},{1,0},{2,3},{3,2},{4,5},{5,4},{6,7},{7,6},{8,9},{9,8},{10,11... | collective-permute-start | bytes 786440 | tf_op jit(solution)/shard_map/ppermute | solution.py:13
  0.7 0.7 %copy-start.2 = (f32[4096]{0:T(1024)S(1)}, f32[4096]{0:T(1024)}, u32[]{:S(2)}) copy-start(f32[4096]{0:T(1024)} %param.4) | copy-start | bytes 49156
  3.0 0.7 %slice-start.1 = ((f32[4096]{0:T(1024)}), f32[2048]{0:T(1024)S(1)}, s32[]{:S(2)}) async-start(f32[4096]{0:T(1024)} %param.4), calls=%async_computation.3 | async-start | bytes 16384 | tf_op jit(solution)/shard_map/slice | solution.py:155
  4.2 0.7 %slice-start = ((f32[4096]{0:T(1024)}), f32[1024]{0:T(1024)S(1)}, s32[]{:S(2)}) async-start(f32[4096]{0:T(1024)} %param.4), calls=%async_computation.2 | async-start | bytes 8192 | tf_op jit(solution)/shard_map/slice | solution.py:155
  6.6 1.0 %copy-start.1 = (f32[2,256,128]{2,1,0:T(8,128)S(1)}, f32[2,256,128]{2,1,0:T(8,128)}, u32[]{:S(2)}) copy-start(f32[2,256,128]{2,1,0:T(8,128)} %param.3) | copy-start | bytes 786436
  11.4 16.4 %all-to-all-start = ((f32[2,256,128]{2,0,1:T(2,128)}), f32[2,256,128]{2,0,1:T(2,128)S(1)}, u32[]{:S(2)}, u32[]{:S(2)}) async-start(f32[2,256,128]{2,0,1:T(2,128)} %copy.46), calls=%async_computation | async-start | bytes 524288 | tf_op jit(solution)/shard_map/all_to_all | solution.py:147
